TPU v7x, 128 devices: a whole 4x4x4 slice. The times are simulated.
128 devices in a mesh: past: 8 (over y, z_lo), second: 16 (over x, z_hi, core).
Axes of the slice: x: 4, y: 4, z: 4 (z_hi: 2, z_lo: 2; z = z_hi * 2 + z_lo), core: 2. Of those that a mesh axis runs over, the one named last changes fastest.
Arguments:
- resident: bfloat16 [24576, 24576], P('past', 'second'), may hold values from -6 to 6
- memory: bfloat16 [2, 384, 24576], P(None, None, 'past'), may hold values from -0.0390625 to 0.0390625
- previous: bfloat16 [2, 384, 24576], P(None, None, 'second'), may hold values from -6 to 6
- inverse_part: float32 [2, 384, 384], replicated, may hold values from -0.3125 to 0.3125
- pair_coupling: float32 [32, 32], replicated, may hold values from 0.000318944 to 0.00318944
Outputs:
- fronts: bfloat16 [2, 384, 24576], P(None, None, 'second')
All inputs are finite; a program needn't handle non-finite values.
Results may differ from a plain program's by a relative error of at most 0.017.
Values may be sent and summed in bfloat16 or wider, within the bound.
No kernel may reach another device: no remote copies, remote signals or barrier semaphores. Data moves between devices by JAX's collectives and lax.ppermute only.
A program may use at most 128 MiB of HBM per device.

v0:
```python
import jax
import jax.numpy as jnp
from jax import lax
from jax.sharding import PartitionSpec as P

step_size = 0.5


def orbital_flip(block, orbitals):
    row_count, col_count = block.shape
    blocks = block.reshape(row_count // orbitals, orbitals, col_count // orbitals, orbitals)
    return blocks.transpose(0, 3, 2, 1).reshape(row_count, col_count)


def solve_front(summed, prior, inverse_block):
    source = prior.astype(jnp.float32) - step_size * summed
    solved = source + jnp.dot(
        inverse_block, source, precision=lax.Precision.HIGHEST, preferred_element_type=jnp.float32
    )
    return solved.astype(jnp.bfloat16)


def self_energy(front, pair_coupling):
    orbitals = pair_coupling.shape[0]
    row_count, col_count = front.shape
    values = front.astype(jnp.float32)
    mirror = orbital_flip(values, orbitals)
    blocks = (values * values * mirror).reshape(
        row_count // orbitals, orbitals, col_count // orbitals, orbitals
    )
    return (
        (blocks * pair_coupling[None, :, None, :])
        .reshape(row_count, col_count)
        .astype(jnp.bfloat16)
    )


def per_device(resident, memory, previous, inverse_part, pair_coupling):

    def advance(memory_row, front_index):
        partial_value = jnp.dot(memory_row, resident, preferred_element_type=jnp.float32)
        summed = lax.psum(partial_value.astype(jnp.bfloat16), "past").astype(jnp.float32)
        prior_cols = previous[front_index]
        return solve_front(summed, prior_cols, inverse_part[front_index])

    front_one = advance(memory[0], 0)
    energy_one = self_energy(front_one, pair_coupling)
    span_cols = memory.shape[2]
    whole_row = lax.all_gather(energy_one, "second", axis=1, tiled=True)
    gathered = lax.dynamic_slice_in_dim(whole_row, lax.axis_index("past") * span_cols, span_cols, 1)
    orbitals = pair_coupling.shape[0]
    memory_next = (
        memory[1].astype(jnp.float32) + orbital_flip(gathered, orbitals).astype(jnp.float32)
    ).astype(jnp.bfloat16)
    front_two = advance(memory_next, 1)
    return jnp.stack([front_one, front_two])


def solution(mesh):
    in_specs = (P("past", "second"), P(None, None, "past"), P(None, None, "second"), P(), P())
    out_specs = P(None, None, "second")
    return jax.shard_map(
        per_device, mesh=mesh, in_specs=in_specs, out_specs=out_specs, check_vma=False
    )
```

profile of v0, /device:TPU:0, one launch (start us, length us, event | category | flops | bytes accessed | tf_op | source)
XLA Modules:
  0.0 406.2 jit_solution(5935509110012505917)
XLA Ops:
  6.5 0.0 copy-start
  6.5 0.0 all-reduce.3.cloned.1.call-start
  6.5 9.2 %convolution_convert_fusion.1 = bf16[384,1536]{1,0:T(8,128)(2,1)} fusion(bf16[3072,1536]{1,0:T(8,128)(2,1)} %param.5, bf16[2,384,3072]{2,1,0:T(8,128)(2,1)} %param.6), kind=kOutput, calls=%fused_computation.9 | convolution fusion | flops 3624468480 | bytes 12976128 | tf_op jit(solution)/shard_map/dot_general | solution.py:41
  15.8 0.0 all-reduce.3.cloned.1.call-update
  15.8 0.0 all-gather.2.cloned.1.call-start
  15.8 0.0 copy-done
  15.9 4.4 %mul.29 = f32[12,32,48,32]{3,2,1,0:T(8,128)} broadcast(f32[32,32]{1,0:T(8,128)S(1)} %copy-done), dimensions={1,3} | broadcast | bytes 2363392 | tf_op jit(solution)/shard_map/mul | solution.py:32
  20.3 6.7 %mul.30 = f32[384,1536]{1,0:T(8,128)S(1)} reshape(f32[12,32,48,32]{3,2,1,0:T(8,128)} %mul.29) | data formatting | bytes 4718592 | tf_op jit(solution)/shard_map/mul | solution.py:32
  27.0 70.5 %all-reduce.3.cloned.1.call-done = bf16[384,1536]{1,0:T(8,128)(2,1)} async-done(((bf16[384,1536]{1,0:T(8,128)(2,1)}), bf16[384,1536]{1,0:T(8,128)(2,1)}) %all-reduce.3.cloned.1.call-update) | async-done | bytes 1179664 | tf_op jit(solution)/shard_map/psum | solution.py:42
  97.5 6.8 %fusion.3 = bf16[384,1536]{1,0:T(8,128)(2,1)S(1)} fusion(bf16[384,1536]{1,0:T(8,128)(2,1)} %all-reduce.3.cloned.1.call-done, bf16[2,384,1536]{2,1,0:T(8,128)(2,1)} %param.7, f32[2,384,384]{2,1,0:T(8,128)} %param.8), kind=kOutput, calls=%fused_computation.6 | convolution fusion | flops 2723807232 | bytes 6488064 | tf_op jit(solution)/shard_map/dot_general | solution.py:17
  104.3 4.9 %reshape.22 = f32[12,32,48,32]{3,2,1,0:T(8,128)} reshape(bf16[384,1536]{1,0:T(8,128)(2,1)S(1)} %fusion.3) | data formatting | bytes 3538944 | tf_op jit(solution)/shard_map/reshape | solution.py:11
  109.2 10.8 %copy.11 = f32[12,32,48,32]{3,2,1,0:T(8,128)} copy(f32[12,32,48,32]{1,2,3,0:T(8,128)} %bitcast.55) | data formatting | bytes 4718592 | tf_op jit(solution)/shard_map/transpose | solution.py:12
  120.0 7.7 %reshape.23 = f32[384,1536]{1,0:T(8,128)} reshape(f32[12,32,48,32]{3,2,1,0:T(8,128)} %copy.11) | data formatting | bytes 4718592 | tf_op jit(solution)/shard_map/reshape | solution.py:12
  127.8 3.3 multiply_convert_fusion
  131.1 0.0 all-gather.2.cloned.1.call-update
  131.1 0.2 all-reduce.5.cloned.1.call-start
  131.3 119.3 %all-gather.2.cloned.1.call-done = bf16[384,24576]{1,0:T(8,128)(2,1)} async-done(((bf16[384,1536]{1,0:T(8,128)(2,1)}), bf16[384,24576]{1,0:T(8,128)(2,1)}) %all-gather.2.cloned.1.call-update) | async-done | bytes 18874384 | tf_op jit(solution)/shard_map/all_gather | solution.py:49
  250.6 4.4 %dynamic-slice_convert_fusion = f32[384,3072]{1,0:T(8,128)} fusion(bf16[384,24576]{1,0:T(8,128)(2,1)} %all-gather.2.cloned.1.call-done, s32[]{:T(128)S(6)} %select_n.3), kind=kLoop, calls=%fused_computation.18 | loop fusion | flops 1179648 | bytes 7077892 | tf_op jit(solution)/shard_map/convert_element_type | solution.py:53
  255.0 12.3 %reshape.28 = f32[12,32,96,32]{3,2,1,0:T(8,128)} reshape(f32[384,3072]{1,0:T(8,128)} %dynamic-slice_convert_fusion) | data formatting | bytes 9437184 | tf_op jit(solution)/shard_map/convert_element_type | solution.py:53
  267.3 22.5 %copy.12 = f32[12,32,96,32]{3,2,1,0:T(8,128)} copy(f32[12,32,96,32]{1,2,3,0:T(8,128)} %bitcast.54) | data formatting | bytes 9437184 | tf_op jit(solution)/shard_map/convert_element_type | solution.py:53
  289.7 14.6 %reshape.27 = f32[384,3072]{1,0:T(8,128)} reshape(f32[12,32,96,32]{3,2,1,0:T(8,128)} %copy.12) | data formatting | bytes 9437184 | tf_op jit(solution)/shard_map/convert_element_type | solution.py:53
  304.3 0.0 copy-start.1
  304.3 10.7 %convolution_convert_fusion = bf16[384,1536]{1,0:T(8,128)(2,1)} fusion(bf16[3072,1536]{1,0:T(8,128)(2,1)} %param.5, f32[384,3072]{1,0:T(8,128)} %reshape.27, bf16[2,384,3072]{2,1,0:T(8,128)(2,1)} %param.6), kind=kOutput, calls=%fused_computation.8 | convolution fusion | flops 3628007424 | bytes 17694720 | tf_op jit(solution)/shard_map/dot_general | solution.py:41
  315.0 0.0 all-reduce.5.cloned.1.call-update
  315.1 77.0 %all-reduce.5.cloned.1.call-done = bf16[384,1536]{1,0:T(8,128)(2,1)} async-done(((bf16[384,1536]{1,0:T(8,128)(2,1)}), bf16[384,1536]{1,0:T(8,128)(2,1)}) %all-reduce.5.cloned.1.call-update) | async-done | bytes 1179664 | tf_op jit(solution)/shard_map/psum | solution.py:42
  392.0 0.0 copy-done.1
  392.0 6.1 %fusion.5 = bf16[1,384,1536]{2,1,0:T(8,128)(2,1)S(1)} fusion(bf16[384,1536]{1,0:T(8,128)(2,1)} %all-reduce.5.cloned.1.call-done, bf16[2,384,1536]{2,1,0:T(8,128)(2,1)S(1)} %copy-done.1, f32[2,384,384]{2,1,0:T(8,128)} %param.8), kind=kOutput, calls=%fused_computation.10 | convolution fusion | flops 2723807232 | bytes 6488064 | tf_op jit(solution)/shard_map/dot_general | solution.py:17
  398.1 1.6 pad_maximum_fusion
Async XLA Ops:
  6.5 9.3 %copy-start = (f32[32,32]{1,0:T(8,128)S(1)}, f32[32,32]{1,0:T(8,128)}, u32[]{:S(2)}) copy-start(f32[32,32]{1,0:T(8,128)} %param.9) | copy-start | bytes 12292
  6.5 91.0 %all-reduce.3.cloned.1.call-start = ((), (), s32[]{:S(2)}) async-start(), calls=%async_computation | async-start | bytes 2359296 | tf_op jit(solution)/shard_map/psum | solution.py:42
  15.8 234.8 %all-gather.2.cloned.1.call-start = ((), (), s32[]{:S(2)}) async-start(), calls=%async_computation.1 | async-start | bytes 20054016 | tf_op jit(solution)/shard_map/all_gather | solution.py:49
  131.1 260.9 %all-reduce.5.cloned.1.call-start = ((), (), s32[]{:S(2)}) async-start(), calls=%async_computation.2 | async-start | bytes 2359296 | tf_op jit(solution)/shard_map/psum | solution.py:42
  304.3 87.7 %copy-start.1 = (bf16[2,384,1536]{2,1,0:T(8,128)(2,1)S(1)}, bf16[2,384,1536]{2,1,0:T(8,128)(2,1)}, u32[]{:S(2)}) copy-start(bf16[2,384,1536]{2,1,0:T(8,128)(2,1)} %param.7) | copy-start | bytes 7077892
Sparse Core Ops, SparseCore 0:
  15.9 81.5 all-reduce.2
  131.2 119.3 all-gather.1
  315.2 76.7 all-reduce.4
where the time goes:
time: 407 us; the launch traced here: 406 us
  waiting for transfers between devices  267 us (66%)
  local copies, waits for them, and re-layouts  83.9 us (21%)
  matrix products  32.8 us (8%)
  between operations  13.1 us (3%)
  other arithmetic  9.31 us (2%)
    psum x2, waiting for transfers between devices, advance(): lax.psum(partial_value.astype(jnp.bfloat16), 'past').astype(jnp.float32)  147 us
    all_gather x1, waiting for transfers between devices, per_device(): whole_row = lax.all_gather(energy_one, 'second', axis=1, tiled=True)  119 us
    convert_element_type x3, local copies, waits for them, and re-layouts, per_device(): orbital_flip(gathered, orbitals).astype(jnp.float32)  49.3 us
    dot_general x2, matrix products, advance(): jnp.dot(memory_row, resident, preferred_element_type=jnp.float32)  19.9 us
    dot_general x2, matrix products, solve_front(): jnp.dot(inverse_block, source, precision=lax.Precision.HIGHEST, preferred...  12.9 us
    mul x2, local copies, waits for them, and re-layouts, self_energy(): blocks * pair_coupling[None, :, None, :]  11.2 us
    transpose x1, local copies, waits for them, and re-layouts, orbital_flip(): return blocks.transpose(0, 3, 2, 1).reshape(row_count, col_count)  10.8 us
  transfers between devices with their start and end apart: 3, of which 3 were waited for; matrix products, arithmetic and copies ran while one was open for 3% of the time, Pallas kernels for 0%

commit v1 on v0

--- a/solution.py
+++ b/solution.py
@@ -46,7 +46,10 @@
     front_one = advance(memory[0], 0)
     energy_one = self_energy(front_one, pair_coupling)
     span_cols = memory.shape[2]
-    whole_row = lax.all_gather(energy_one, "second", axis=1, tiled=True)
+    peers = lax.axis_size("second")
+    pieces = jnp.stack([energy_one for _ in range(peers)])
+    pieces = lax.all_to_all(pieces, "second", split_axis=0, concat_axis=0)
+    whole_row = jnp.concatenate(pieces, axis=1)
     gathered = lax.dynamic_slice_in_dim(whole_row, lax.axis_index("past") * span_cols, span_cols, 1)
     orbitals = pair_coupling.shape[0]
     memory_next = (

time: 407 us -> 619 us (1.52)
  waiting for transfers between devices: 267 us -> 457 us
  local copies, waits for them, and re-layouts: 83.9 us -> 98.6 us
  starting transfers between devices: 0.27 us -> 6.77 us
    all_to_all x0 -> x1, waiting for transfers between devices: none -> 306 us  [per_device(): pieces = lax.all_to_all(pieces, 'second', split_axis=0, concat_axis=0)]
    all_gather x1 -> x0, waiting for transfers between devices: 119 us -> none  [per_device(): whole_row = lax.all_gather(energy_one, 'second', axis=1, tiled=True)]
    another operation x0 -> x1, local copies, waits for them, and re-layouts: none -> 6.94 us  [per_device(): pieces = jnp.stack([energy_one for _ in range(peers)])]
    all_to_all x0 -> x1, starting transfers between devices: none -> 6.72 us  [per_device(): pieces = lax.all_to_all(pieces, 'second', split_axis=0, concat_axis=0)]
    convert_element_type x3 -> x4, local copies, waits for them, and re-layouts: 49.3 us -> 55.4 us  [per_device(): orbital_flip(gathered, orbitals).astype(jnp.float32)]
  transfers between devices with their start and end apart: 3 -> 3, of which waited for: 3 -> 3; matrix products, arithmetic and copies ran while one was open for 3% -> 2% of each run, Pallas kernels for 0% -> 0%
where the time goes in v1:
time: 619 us; the launch traced here: 617 us
  waiting for transfers between devices  457 us (74%)
  local copies, waits for them, and re-layouts  98.6 us (16%)
  matrix products  32.8 us (5%)
  between operations  13.5 us (2%)
  other arithmetic  9.04 us (1%)
  starting transfers between devices  6.77 us (1%)
    all_to_all x1, waiting for transfers between devices, per_device(): pieces = lax.all_to_all(pieces, 'second', split_axis=0, concat_axis=0)  306 us
    psum x2, waiting for transfers between devices, advance(): lax.psum(partial_value.astype(jnp.bfloat16), 'past').astype(jnp.float32)  150 us
    convert_element_type x4, local copies, waits for them, and re-layouts, per_device(): orbital_flip(gathered, orbitals).astype(jnp.float32)  55.4 us
    dot_general x2, matrix products, advance(): jnp.dot(memory_row, resident, preferred_element_type=jnp.float32)  19.9 us
    dot_general x2, matrix products, solve_front(): jnp.dot(inverse_block, source, precision=lax.Precision.HIGHEST, preferred...  12.9 us
  transfers between devices with their start and end apart: 3, of which 3 were waited for; matrix products, arithmetic and copies ran while one was open for 2% of the time, Pallas kernels for 0%

profile of v1, /device:TPU:0, one launch (start us, length us, event | category | flops | bytes accessed | tf_op | source)
XLA Modules:
  0.0 617.2 jit_solution(13687921291772841776)
XLA Ops:
  6.5 0.0 copy-start
  6.5 0.0 all-reduce.3.cloned.1.call-start
  6.5 9.2 %convolution_convert_fusion.1 = bf16[384,1536]{1,0:T(8,128)(2,1)} fusion(bf16[3072,1536]{1,0:T(8,128)(2,1)} %param.5, bf16[2,384,3072]{2,1,0:T(8,128)(2,1)} %param.6), kind=kOutput, calls=%fused_computation.9 | convolution fusion | flops 3624468480 | bytes 12976128 | tf_op jit(solution)/shard_map/dot_general | solution.py:41
  15.8 0.0 all-reduce.3.cloned.1.call-update
  15.8 0.0 copy-done
  15.8 4.4 mul.29
  20.2 6.7 %mul.30 = f32[384,1536]{1,0:T(8,128)S(1)} reshape(f32[12,32,48,32]{3,2,1,0:T(8,128)} %mul.29) | data formatting | bytes 4718592 | tf_op jit(solution)/shard_map/mul | solution.py:32
  27.0 70.6 %all-reduce.3.cloned.1.call-done = bf16[384,1536]{1,0:T(8,128)(2,1)} async-done(((bf16[384,1536]{1,0:T(8,128)(2,1)}), bf16[384,1536]{1,0:T(8,128)(2,1)}) %all-reduce.3.cloned.1.call-update) | async-done | bytes 1179664 | tf_op jit(solution)/shard_map/psum | solution.py:42
  97.5 6.8 %fusion.3 = bf16[384,1536]{1,0:T(8,128)(2,1)S(1)} fusion(bf16[384,1536]{1,0:T(8,128)(2,1)} %all-reduce.3.cloned.1.call-done, bf16[2,384,1536]{2,1,0:T(8,128)(2,1)} %param.7, f32[2,384,384]{2,1,0:T(8,128)} %param.8), kind=kOutput, calls=%fused_computation.6 | convolution fusion | flops 2723807232 | bytes 6488064 | tf_op jit(solution)/shard_map/dot_general | solution.py:17
  104.3 4.9 reshape.30
  109.2 10.8 %copy.10 = f32[12,32,48,32]{3,2,1,0:T(8,128)} copy(f32[12,32,48,32]{1,2,3,0:T(8,128)} %bitcast.58) | data formatting | bytes 4718592 | tf_op jit(solution)/shard_map/transpose | solution.py:12
  120.0 7.7 %reshape.31 = f32[384,1536]{1,0:T(8,128)} reshape(f32[12,32,48,32]{3,2,1,0:T(8,128)} %copy.10) | data formatting | bytes 4718592 | tf_op jit(solution)/shard_map/reshape | solution.py:12
  127.7 3.3 multiply_convert_fusion
  131.0 1.7 copy.11
  132.7 6.9 %stack.9 = bf16[16,384,1536]{1,2,0:T(8,128)(2,1)} broadcast(bf16[384,1536]{0,1:T(8,128)(2,1)S(1)} %copy.11), dimensions={1,2} | broadcast | bytes 20054016 | tf_op jit(solution)/shard_map/stack | solution.py:50
  139.7 6.7 %all-to-all-start = ((bf16[16,384,1536]{1,2,0:T(8,128)(2,1)}), bf16[16,384,1536]{1,2,0:T(8,128)(2,1)}, u32[]{:S(2)}, u32[]{:S(2)}) async-start(bf16[16,384,1536]{1,2,0:T(8,128)(2,1)} %stack.9), calls=%async_computation | async-start | bytes 37748736 | tf_op jit(solution)/shard_map/all_to_all | solution.py:51
  146.4 0.0 all-reduce.5.cloned.1.call-start
  146.5 306.4 %all-to-all-done = bf16[16,384,1536]{1,2,0:T(8,128)(2,1)} async-done(((bf16[16,384,1536]{1,2,0:T(8,128)(2,1)}), bf16[16,384,1536]{1,2,0:T(8,128)(2,1)}, u32[]{:S(2)}, u32[]{:S(2)}) %all-to-all-start) | async-done | bytes 18874400 | tf_op jit(solution)/shard_map/all_to_all | solution.py:51
  452.8 4.1 dynamic-slice_convert_fusion
  457.0 6.0 copy.12
  463.0 12.3 %reshape.38 = f32[12,32,96,32]{3,2,1,0:T(8,128)} reshape(f32[384,3072]{1,0:T(8,128)} %copy.12) | data formatting | bytes 9437184 | tf_op jit(solution)/shard_map/convert_element_type | solution.py:56
  475.3 22.5 %copy.13 = f32[12,32,96,32]{3,2,1,0:T(8,128)} copy(f32[12,32,96,32]{1,2,3,0:T(8,128)} %bitcast.57) | data formatting | bytes 9437184 | tf_op jit(solution)/shard_map/convert_element_type | solution.py:56
  497.8 14.6 %reshape.37 = f32[384,3072]{1,0:T(8,128)} reshape(f32[12,32,96,32]{3,2,1,0:T(8,128)} %copy.13) | data formatting | bytes 9437184 | tf_op jit(solution)/shard_map/convert_element_type | solution.py:56
  512.4 0.0 copy-start.1
  512.4 10.7 %convolution_convert_fusion = bf16[384,1536]{1,0:T(8,128)(2,1)} fusion(bf16[3072,1536]{1,0:T(8,128)(2,1)} %param.5, f32[384,3072]{1,0:T(8,128)} %reshape.37, bf16[2,384,3072]{2,1,0:T(8,128)(2,1)} %param.6), kind=kOutput, calls=%fused_computation.8 | convolution fusion | flops 3628007424 | bytes 17694720 | tf_op jit(solution)/shard_map/dot_general | solution.py:41
  523.1 0.0 all-reduce.5.cloned.1.call-update
  523.1 79.6 %all-reduce.5.cloned.1.call-done = bf16[384,1536]{1,0:T(8,128)(2,1)} async-done(((bf16[384,1536]{1,0:T(8,128)(2,1)}), bf16[384,1536]{1,0:T(8,128)(2,1)}) %all-reduce.5.cloned.1.call-update) | async-done | bytes 1179664 | tf_op jit(solution)/shard_map/psum | solution.py:42
  602.7 0.0 copy-done.1
  602.7 6.1 fusion.5
  608.7 1.6 pad_maximum_fusion
Async XLA Ops:
  6.5 9.3 %copy-start = (f32[32,32]{1,0:T(8,128)S(1)}, f32[32,32]{1,0:T(8,128)}, u32[]{:S(2)}) copy-start(f32[32,32]{1,0:T(8,128)} %param.9) | copy-start | bytes 12292
  6.5 91.0 %all-reduce.3.cloned.1.call-start = ((), (), s32[]{:S(2)}) async-start(), calls=%async_computation.1 | async-start | bytes 2359296 | tf_op jit(solution)/shard_map/psum | solution.py:42
  139.7 313.2 %all-to-all-start = ((bf16[16,384,1536]{1,2,0:T(8,128)(2,1)}), bf16[16,384,1536]{1,2,0:T(8,128)(2,1)}, u32[]{:S(2)}, u32[]{:S(2)}) async-start(bf16[16,384,1536]{1,2,0:T(8,128)(2,1)} %stack.9), calls=%async_computation | async-start | bytes 37748736 | tf_op jit(solution)/shard_map/all_to_all | solution.py:51
  146.4 456.2 %all-reduce.5.cloned.1.call-start = ((), (), s32[]{:S(2)}) async-start(), calls=%async_computation.2 | async-start | bytes 2359296 | tf_op jit(solution)/shard_map/psum | solution.py:42
  512.4 90.3 %copy-start.1 = (bf16[2,384,1536]{2,1,0:T(8,128)(2,1)S(1)}, bf16[2,384,1536]{2,1,0:T(8,128)(2,1)}, u32[]{:S(2)}) copy-start(bf16[2,384,1536]{2,1,0:T(8,128)(2,1)} %param.7) | copy-start | bytes 7077892
Sparse Core Ops, SparseCore 0:
  15.9 81.5 all-reduce.2
  523.2 79.3 all-reduce.4
